TPU v7x, 32 devices: a whole 2x2x4 slice. The times are simulated.
32 devices in a mesh: parts: 2 (over y), seq: 4 (over z), head: 4 (over x, core).
Axes of the slice: x: 2, y: 2, z: 4, core: 2. Of those that a mesh axis runs over, the one named last changes fastest.
Arguments:
- queries: bfloat16 [256, 8192], P(('parts', 'seq'), 'head'), parts along dimension 0, may hold values from -110 to 110
- root_keys: bfloat16 [16384, 1024], P(('parts', 'seq'), 'head'), parts along dimension 0, may hold values from -6 to 6
- root_values: bfloat16 [16384, 1024], P(('parts', 'seq'), 'head'), parts along dimension 0, may hold values from -6 to 6
- branch_keys: bfloat16 [16, 2048, 1024], P(('parts', 'seq'), None, 'head'), parts along dimension 0, may hold values from -6 to 6
- branch_values: bfloat16 [16, 2048, 1024], P(('parts', 'seq'), None, 'head'), parts along dimension 0, may hold values from -6 to 6
- branch_id: int32 [256, 1], P('parts'), parts along dimension 0, may hold values from 0 to 7; in each aligned block of 128 rows (0 to 127, 128 to 255, ...) at most 32 rows name the same one
- doc_len: int32 [16], P('parts'), parts along dimension 0, may hold values from 1 to 2048, 10240 in all
Outputs:
- attended: bfloat16 [256, 8192], P(('parts', 'seq'), 'head'), parts along dimension 0
There are 2 independent parts, one for each index of `parts`. A program takes and returns all parts, laid end to end along the dimension named above; each array names one. Nothing has to cross between parts.
Inputs may be any that keep to these rules, and one draw needn't show every extreme that they name: `branch_id`: each of the 8 branches is named by at most 32 rows, a bound that some block reaches. `doc_len`: the 8 lengths of ONE part sum to 10240 and the largest of them is exactly 2048; the printed array holds all parts end to end, so its whole sum is that total times the number of parts.
All inputs are finite; a program needn't handle non-finite values.
Results may differ from a plain program's by a relative error of at most 0.008.
Values may be sent and summed in bfloat16 or wider, within the bound.
A program may use at most 64 MiB of HBM per device.

v0:
```python
import jax
import jax.numpy as jnp
from jax import lax
from jax.sharding import PartitionSpec as P

QHEADS = 64
KVHEADS = 8
HEAD_DIM = 128


masked_score = -1e30


def attend(query_head_rows, key_tile_rows, value_tile_rows, usable):
    logit_scale = HEAD_DIM ** (-0.5)
    logit_scores = (
        jnp.einsum(
            "mfsa,nfa->mfsn", query_head_rows, key_tile_rows, preferred_element_type=jnp.float32
        )
        * logit_scale
    )
    keep = usable[:, None, None, :]
    logit_scores = jnp.where(keep, logit_scores, masked_score)
    row_max = jnp.max(logit_scores, axis=-1)
    softmax_weights = jnp.where(keep, jnp.exp(logit_scores - row_max[..., None]), 0.0)
    row_sum = jnp.sum(softmax_weights, axis=-1)
    weighted_values = jnp.einsum(
        "taoz,zah->taoh",
        softmax_weights.astype(jnp.bfloat16),
        value_tile_rows,
        preferred_element_type=jnp.float32,
    )
    return (row_max, row_sum, weighted_values)


def combine(first, second):
    row_max = jnp.maximum(first[0], second[0])
    factor_a = jnp.exp(first[0] - row_max)
    factor_b = jnp.exp(second[0] - row_max)
    return (
        row_max,
        first[1] * factor_a + second[1] * factor_b,
        first[2] * factor_a[..., None] + second[2] * factor_b[..., None],
    )


def body(queries, root_keys, root_values, branch_keys, branch_values, branch_id, doc_len):
    gathered = lax.all_gather(queries, "seq", axis=0, tiled=True)
    row_count = gathered.shape[0]
    kv_local = root_keys.shape[1] // HEAD_DIM
    group = QHEADS // KVHEADS
    query_head_rows = gathered.reshape(row_count, kv_local, group, HEAD_DIM)
    block_len = min(1024, root_keys.shape[0])
    block_count = root_keys.shape[0] // block_len
    key_blocks = root_keys.reshape(block_count, block_len, kv_local, HEAD_DIM)
    value_blocks = root_values.reshape(block_count, block_len, kv_local, HEAD_DIM)
    starts = (
        jnp.full((row_count, kv_local, group), masked_score, jnp.float32),
        jnp.zeros((row_count, kv_local, group), jnp.float32),
        jnp.zeros((row_count, kv_local, group, HEAD_DIM), jnp.float32),
    )

    def root_step(carry, pair):
        usable = jnp.ones((1, block_len), bool)
        return (combine(carry, attend(query_head_rows, pair[0], pair[1], usable)), None)

    root_part, _ = lax.scan(root_step, starts, (key_blocks, value_blocks))
    seq_count = lax.axis_size("seq")
    row_dev = row_count // seq_count
    branch_dev = branch_keys.shape[0]
    most_rows = 2 * row_dev // branch_dev
    branch_len = branch_keys.shape[1]
    branch_part = starts
    for local_branch in range(branch_dev):
        branch = lax.axis_index("seq") * branch_dev + local_branch
        chosen = jnp.argsort((branch_id[:, 0] != branch).astype(jnp.int32), stable=True)[:most_rows]
        row_live = branch_id[chosen, 0] == branch
        key_live = jnp.arange(branch_len) < doc_len[branch]
        usable = row_live[:, None] & key_live[None, :]
        key_tile_rows = branch_keys[local_branch].reshape(branch_len, kv_local, HEAD_DIM)
        value_tile_rows = branch_values[local_branch].reshape(branch_len, kv_local, HEAD_DIM)
        result = attend(query_head_rows[chosen], key_tile_rows, value_tile_rows, usable)
        target = jnp.where(row_live, chosen, row_count)
        branch_part = (
            branch_part[0].at[target].set(result[0], mode="drop"),
            branch_part[1].at[target].set(result[1], mode="drop"),
            branch_part[2].at[target].set(result[2], mode="drop"),
        )
    local_part = combine(root_part, branch_part)
    shares = (
        lax.all_to_all(local_part[0][None], "seq", split_axis=1, concat_axis=0, tiled=True),
        lax.all_to_all(local_part[1][None], "seq", split_axis=1, concat_axis=0, tiled=True),
        lax.all_to_all(local_part[2][None], "seq", split_axis=1, concat_axis=0, tiled=True),
    )
    row_max = jnp.max(shares[0], axis=0)
    factor = jnp.exp(shares[0] - row_max[None])
    row_sum = jnp.sum(shares[1] * factor, axis=0)
    weighted_values = jnp.sum(shares[2] * factor[..., None], axis=0)
    attended = weighted_values / row_sum[..., None]
    return attended.astype(jnp.bfloat16).reshape(row_dev, kv_local * group * HEAD_DIM)


def solution(mesh):
    in_specs = (
        P(("parts", "seq"), "head"),
        P(("parts", "seq"), "head"),
        P(("parts", "seq"), "head"),
        P(("parts", "seq"), None, "head"),
        P(("parts", "seq"), None, "head"),
        P("parts", None),
        P("parts"),
    )
    out_specs = P(("parts", "seq"), "head")
    return jax.shard_map(body, mesh=mesh, in_specs=in_specs, out_specs=out_specs, check_vma=False)
```

profile of v0, /device:TPU:0, one launch (start us, length us, event | category | flops | bytes accessed | tf_op | source)
XLA Modules:
  0.0 124.0 jit_solution(15404459378698408892)
XLA Ops:
  0.0 17.7 %all_gather.3 = bf16[128,2048]{1,0:T(8,128)(2,1)S(1)} all-gather(bf16[32,2048]{1,0:T(8,128)(2,1)} %param.9), channel_id=1, replica_groups=mesh['parts'=2,'seq'=4,'head'=4] {'seq'}, dimensions={0}, use_global_device_ids=true | all-gather | bytes 655360 | tf_op jit(solution)/shard_map/all_gather | solution.py:48
  19.4 2.5 %sort.31 = (s32[128]{0:T(128)}, s32[128]{0:T(128)S(1)}) sort(s32[128]{0:T(128)S(1)} %get-tuple-element.139, s32[128]{0:T(128)S(1)} %iota.17), dimensions={0}, to_apply=%region_4.5 | sort | flops 896 | bytes 2048 | tf_op jit(solution)/shard_map/jit(argsort)/sort | solution.py:76
  23.3 2.5 %sort.32 = (s32[128]{0:T(128)}, s32[128]{0:T(128)S(1)}) sort(s32[128]{0:T(128)S(1)} %get-tuple-element.138, s32[128]{0:T(128)S(1)} %iota.19), dimensions={0}, to_apply=%region_7.8 | sort | flops 896 | bytes 2048 | tf_op jit(solution)/shard_map/jit(argsort)/sort | solution.py:76
  31.9 2.2 %reshape.114 = bf16[2,1024,2,128]{3,2,1,0:T(2,128)(2,1)} reshape(bf16[2048,256]{1,0:T(8,128)(2,1)} %param.11) | data formatting | bytes 2097152 | tf_op jit(solution)/shard_map/reshape | solution.py:56
  34.1 13.9 %while.15 = (s32[]{:T(128)}, f32[128,2,8]{0,2,1:T(8,128)S(1)}, f32[128,2,8]{0,2,1:T(8,128)S(1)}, f32[128,2,8,128]{0,3,2,1:T(8,128)S(1)}, bf16[2,1024,2,128]{3,2,...) while((s32[]{:T(128)}, f32[128,2,8]{0,2,1:T(8,128)S(1)}, ...), condition=%wide.region_3.4_spmd.clone, body=%wide.region_0.3_spmd.clone.sunk | while | flops 1091579904 | bytes 32096368 | solution.py:67
  34.1 1.9 %constant_dynamic-slice_fusion.3 = (bf16[1,1024,2,128]{3,2,1,0:T(2,128)(2,1)S(1)}, bf16[1,1024,2,128]{3,2,1,0:T(2,128)(2,1)S(1)}) fusion(bf16[2,1024,2,128]{3,2,1,0:T(2,128)(2,1)} %get-tuple-element.227, s32[]{:T(128)S(6)} %copy.152, bf16[2,1024,2,128]{3,2,1,0:T(2,128)(2,1)} %get-tuple-element.225), kind=kLoop, calls=%fused_computation.30.clone.1 | loop fusion | bytes 2097156 | tf_op jit(solution)/shard_map/while/body/jit(dynamic_index_in_dim)/dynamic_slice | solution.py:67
  39.1 1.9 %fusion.73 = f32[128,2,8,128]{0,3,2,1:T(8,128)S(1)} fusion(f32[2,1024,128,8]{2,1,3,0:T(8,128)S(1)} %get-tuple-element.196, f32[128,2,8]{0,2,1:T(8,128)S(1)} %get-tuple-element.197, f32[128,2,8,128]{0,3,2,1:T(8,128)S(1)} %get-tuple-element.215, bf16[1,1024,2,128]{1,3,2,0:T(8,128)(2,1)S(1)} %copy.145, f32[128,2,8]{0,2,1:T(8,128)S(1)} %get-tuple-element.201, ...), kind=kOutput, calls=%fused_computation.20.clone.1 | convolution fusion | flops 544210944 | bytes 11034625 | tf_op jit(solution)/shard_map/while/body/eval_jaxpr/taoz,zah->taoh/dot_general | solution.py:27
  41.0 1.9 %constant_dynamic-slice_fusion.3 = (bf16[1,1024,2,128]{3,2,1,0:T(2,128)(2,1)S(1)}, bf16[1,1024,2,128]{3,2,1,0:T(2,128)(2,1)S(1)}) fusion(bf16[2,1024,2,128]{3,2,1,0:T(2,128)(2,1)} %get-tuple-element.227, s32[]{:T(128)S(6)} %copy.152, bf16[2,1024,2,128]{3,2,1,0:T(2,128)(2,1)} %get-tuple-element.225), kind=kLoop, calls=%fused_computation.30.clone.1 | loop fusion | bytes 2097156 | tf_op jit(solution)/shard_map/while/body/jit(dynamic_index_in_dim)/dynamic_slice | solution.py:67
  46.1 1.9 %fusion.73 = f32[128,2,8,128]{0,3,2,1:T(8,128)S(1)} fusion(f32[2,1024,128,8]{2,1,3,0:T(8,128)S(1)} %get-tuple-element.196, f32[128,2,8]{0,2,1:T(8,128)S(1)} %get-tuple-element.197, f32[128,2,8,128]{0,3,2,1:T(8,128)S(1)} %get-tuple-element.215, bf16[1,1024,2,128]{1,3,2,0:T(8,128)(2,1)S(1)} %copy.145, f32[128,2,8]{0,2,1:T(8,128)S(1)} %get-tuple-element.201, ...), kind=kOutput, calls=%fused_computation.20.clone.1 | convolution fusion | flops 544210944 | bytes 11034625 | tf_op jit(solution)/shard_map/while/body/eval_jaxpr/taoz,zah->taoh/dot_general | solution.py:27
  48.0 2.7 %fusion.54 = (bf16[1,2048,256]{2,1,0:T(8,128)(2,1)S(1)}, bf16[1,2048,256]{2,1,0:T(8,128)(2,1)}) fusion(bf16[2,2048,256]{2,1,0:T(8,128)(2,1)} %param.12), kind=kLoop, calls=%fused_computation.93 | loop fusion | bytes 4194304 | tf_op jit(solution)/shard_map/slice | solution.py:80
  54.2 1.5 %fusion.24 = f32[32,2,8]{2,0,1:T(8,128)S(1)} fusion(f32[2,32,8,2048]{3,2,1,0:T(8,128)S(1)} %get-tuple-element.141, f32[32,2,8]{2,0,1:T(8,128)S(1)} %get-tuple-element.140, pred[32,2048]{1,0:T(8,128)(4,1)S(1)} %broadcast_and_fusion.1), kind=kLoop, calls=%fused_computation.43 | loop fusion | flops 5242368 | bytes 4263936 | tf_op jit(solution)/shard_map/reduce_sum | solution.py:26
  57.1 1.9 %copy-done.2 = f32[2,32,8,2048]{3,2,1,0:T(8,128)} copy-done((f32[2,32,8,2048]{3,2,1,0:T(8,128)}, f32[2,32,8,2048]{3,2,1,0:T(8,128)S(1)}, u32[]{:S(2)}) %copy-start.2) | copy-done | bytes 4194328
  60.6 1.6 %scatter_fusion = f32[128,2,8]{2,1,0:T(2,128)S(1)} fusion(f32[128,2,8]{2,1,0:T(2,128)S(1)} %broadcast_in_dim.99, s32[32]{0:T(128)S(1)} %copy-done.10, f32[32,2,8]{2,1,0:T(2,128)S(1)} %copy.83), kind=kCustom, calls=%fused_computation.4 | custom fusion | bytes 6272 | tf_op jit(solution)/shard_map/scatter | solution.py:85
  62.2 1.7 %scatter_fusion.1 = f32[128,2,8]{2,1,0:T(2,128)S(1)} fusion(f32[128,2,8]{2,1,0:T(2,128)S(1)} %scatter_fusion, s32[32]{0:T(128)S(1)} %copy-done.12, f32[32,2,8]{2,1,0:T(2,128)S(1)} %copy.88), kind=kCustom, calls=%fused_computation.5 | custom fusion | bytes 6272 | tf_op jit(solution)/shard_map/scatter | solution.py:85
  64.1 1.6 %scatter_fusion.4 = f32[128,2,8]{2,1,0:T(2,128)S(1)} fusion(f32[128,2,8]{2,1,0:T(2,128)S(1)} %broadcast_in_dim.100, s32[32]{0:T(128)S(1)} %copy-done.10, f32[32,2,8]{2,1,0:T(2,128)S(1)} %copy.102), kind=kCustom, calls=%fused_computation.8 | custom fusion | bytes 6272 | tf_op jit(solution)/shard_map/scatter | solution.py:86
  68.2 5.5 %all-to-all-start.2 = ((f32[4,1,512]{2,1,0:T(1,128)}), f32[4,1,512]{2,1,0:T(1,128)S(1)}, u32[]{:S(2)}, u32[]{:S(2)}) async-start(f32[4,1,512]{2,1,0:T(1,128)} %reshape.221), calls=%async_computation.2 | async-start | bytes 16384 | tf_op jit(solution)/shard_map/all_to_all | solution.py:92
  73.7 1.7 %fusion.55 = (bf16[1,2048,256]{2,1,0:T(8,128)(2,1)S(1)}, bf16[1,2048,256]{2,1,0:T(8,128)(2,1)S(1)}) fusion(bf16[2,2048,256]{2,1,0:T(8,128)(2,1)} %param.13), kind=kLoop, calls=%fused_computation.94 | loop fusion | bytes 4194304 | tf_op jit(solution)/shard_map/slice | solution.py:81
  77.6 4.1 %fusion.36 = f32[32,2,8,128]{3,2,0,1:T(8,128)} fusion(bf16[2048,2,128,1]{0,2,3,1:T(8,128)(2,1)S(1)} %bitcast.148, f32[2,32,8,2048]{3,2,1,0:T(8,128)} %copy-done.1, f32[32,2,8]{2,0,1:T(8,128)S(1)} %copy-done.7, pred[32,2048]{1,0:T(8,128)(4,1)S(1)} %broadcast_and_fusion.1), kind=kOutput, calls=%fused_computation.53 | convolution fusion | flops 273678336 | bytes 5572608 | tf_op jit(solution)/shard_map/taoz,zah->taoh/dot_general | solution.py:27
  84.8 1.6 %scatter_fusion.2 = f32[128,2,8,128]{3,2,1,0:T(8,128)S(1)} fusion(f32[128,2,8,128]{3,2,1,0:T(8,128)S(1)} %broadcast_in_dim.101, s32[32]{0:T(128)S(1)} %copy-done.11, f32[32,2,8,128]{3,2,1,0:T(8,128)S(1)} %copy.94), kind=kCustom, calls=%fused_computation.6 | custom fusion | bytes 786560 | tf_op jit(solution)/shard_map/scatter | solution.py:87
  87.9 5.2 %all-to-all-start.1 = ((f32[4,1,512]{2,1,0:T(1,128)}), f32[4,1,512]{2,1,0:T(1,128)S(1)}, u32[]{:S(2)}, u32[]{:S(2)}) async-start(f32[4,1,512]{2,1,0:T(1,128)} %reshape.219), calls=%async_computation.1 | async-start | bytes 16384 | tf_op jit(solution)/shard_map/all_to_all | solution.py:91
  93.1 1.6 %add_bitcast_fusion = f32[1,128,2,8,128]{4,3,2,0,1:T(8,128)} fusion(f32[128,2,8,128]{3,2,1,0:T(8,128)S(1)} %scatter_fusion.3, f32[128,2,8,128]{3,2,1,0:T(8,128)S(1)} %copy.91, f32[128,2,8]{2,1,0:T(2,128)S(1)} %copy.99, f32[128,2,8]{2,1,0:T(2,128)S(1)} %copy.90), kind=kLoop, calls=%fused_computation.56 | loop fusion | flops 786432 | bytes 3162112 | tf_op jit(solution)/shard_map/broadcast_in_dim | solution.py:93
  94.7 4.0 %all-to-all-done.1 = f32[4,1,512]{2,1,0:T(1,128)S(1)} async-done(((f32[4,1,512]{2,1,0:T(1,128)}), f32[4,1,512]{2,1,0:T(1,128)S(1)}, u32[]{:S(2)}, u32[]{:S(2)}) %all-to-all-start.1) | async-done | bytes 8224 | tf_op jit(solution)/shard_map/all_to_all | solution.py:91
  98.7 3.5 %all-to-all-start = ((f32[1,128,2,8,128]{4,3,2,0,1:T(8,128)}), f32[1,128,2,8,128]{4,3,2,0,1:T(8,128)S(1)}, u32[]{:S(2)}, u32[]{:S(2)}) async-start(f32[1,128,2,8,128]{4,3,2,0,1:T(8,128)} %add_bitcast_fusion), calls=%async_computation | async-start | bytes 2097152 | tf_op jit(solution)/shard_map/all_to_all | solution.py:93
  104.8 18.0 %all-to-all-done = f32[1,128,2,8,128]{4,3,2,0,1:T(8,128)S(1)} async-done(((f32[1,128,2,8,128]{4,3,2,0,1:T(8,128)}), f32[1,128,2,8,128]{4,3,2,0,1:T(8,128)S(1)}, u32[]{:S(2)}, u32[]{:S(2)}) %all-to-all-start) | async-done | bytes 1048608 | tf_op jit(solution)/shard_map/all_to_all | solution.py:93
  (104 shorter events, 34.6 us)
Async XLA Ops:
  0.0 22.0 %copy-start = (s32[128,1]{0,1:T(1,128)S(1)}, s32[128,1]{0,1:T(1,128)}, u32[]{:S(2)}) copy-start(s32[128,1]{0,1:T(1,128)} %param.14) | copy-start | bytes 1540
  0.0 27.1 %copy-start.15 = (s32[8]{0:T(128)S(1)}, s32[8]{0:T(128)}, u32[]{:S(2)}) copy-start(s32[8]{0:T(128)} %param.15) | copy-start | bytes 100
  0.0 30.7 %copy-start.4 = (bf16[2048,256]{1,0:T(8,128)(2,1)S(1)}, bf16[2048,256]{1,0:T(8,128)(2,1)}, u32[]{:S(2)}) copy-start(bf16[2048,256]{1,0:T(8,128)(2,1)} %param.10) | copy-start | bytes 3145732
  52.9 2.8 %copy-start.9 = (pred[2048]{0:T(1024)(128)(4,1)S(1)}, pred[2048]{0:T(1024)(128)(4,1)}, u32[]{:S(2)}) copy-start(pred[2048]{0:T(1024)(128)(4,1)} %iota_compare_fusion) | copy-start | bytes 6148
  52.9 2.8 %copy-start.14 = (pred[32]{0:T(512)(128)(4,1)S(1)}, pred[32]{0:T(512)(128)(4,1)}, u32[]{:S(2)}) copy-start(pred[32]{0:T(512)(128)(4,1)} %get-tuple-element.120) | copy-start | bytes 100
  54.1 1.6 %copy-start.6 = (f32[32,2,8]{2,0,1:T(8,128)}, f32[32,2,8]{2,0,1:T(8,128)S(1)}, u32[]{:S(2)}) copy-start(f32[32,2,8]{2,0,1:T(8,128)S(1)} %get-tuple-element.140) | copy-start | bytes 6148
  54.1 3.0 %copy-start.1 = (f32[2,32,8,2048]{3,2,1,0:T(8,128)}, f32[2,32,8,2048]{3,2,1,0:T(8,128)S(1)}, u32[]{:S(2)}) copy-start(f32[2,32,8,2048]{3,2,1,0:T(8,128)S(1)} %get-tuple-element.141) | copy-start | bytes 12582916
  55.9 4.8 %copy-start.10 = (s32[32]{0:T(128)S(1)}, s32[32]{0:T(128)}, u32[]{:S(2)}) copy-start(s32[32]{0:T(128)} %get-tuple-element.123) | copy-start | bytes 388
  55.9 6.3 %copy-start.12 = (s32[32]{0:T(128)S(1)}, s32[32]{0:T(128)}, u32[]{:S(2)}) copy-start(s32[32]{0:T(128)} %get-tuple-element.119) | copy-start | bytes 388
  57.1 2.0 %copy-start.2 = (f32[2,32,8,2048]{3,2,1,0:T(8,128)}, f32[2,32,8,2048]{3,2,1,0:T(8,128)S(1)}, u32[]{:S(2)}) copy-start(f32[2,32,8,2048]{3,2,1,0:T(8,128)S(1)} %get-tuple-element.143) | copy-start | bytes 12582916
  68.2 19.7 %all-to-all-start.2 = ((f32[4,1,512]{2,1,0:T(1,128)}), f32[4,1,512]{2,1,0:T(1,128)S(1)}, u32[]{:S(2)}, u32[]{:S(2)}) async-start(f32[4,1,512]{2,1,0:T(1,128)} %reshape.221), calls=%async_computation.2 | async-start | bytes 16384 | tf_op jit(solution)/shard_map/all_to_all | solution.py:92
  73.7 3.8 %copy-start.7 = (f32[32,2,8]{2,0,1:T(8,128)S(1)}, f32[32,2,8]{2,0,1:T(8,128)}, u32[]{:S(2)}) copy-start(f32[32,2,8]{2,0,1:T(8,128)} %copy-done.6) | copy-start | bytes 6148
  77.5 4.2 %copy-start.3 = (f32[2,32,8,2048]{3,2,1,0:T(8,128)S(1)}, f32[2,32,8,2048]{3,2,1,0:T(8,128)}, u32[]{:S(2)}) copy-start(f32[2,32,8,2048]{3,2,1,0:T(8,128)} %copy-done.2) | copy-start | bytes 12582916
  77.6 4.2 %copy-start.5 = (bf16[1,2048,256]{1,2,0:T(8,128)(2,1)S(1)}, bf16[1,2048,256]{1,2,0:T(8,128)(2,1)}, u32[]{:S(2)}) copy-start(bf16[1,2048,256]{1,2,0:T(8,128)(2,1)} %copy.126) | copy-start | bytes 3145732
  81.7 1.7 %copy-start.8 = (f32[32,2,8,128]{3,2,0,1:T(8,128)S(1)}, f32[32,2,8,128]{3,2,0,1:T(8,128)}, u32[]{:S(2)}) copy-start(f32[32,2,8,128]{3,2,0,1:T(8,128)} %fusion.36) | copy-start | bytes 786436
  82.9 1.9 %copy-start.11 = (s32[32]{0:T(128)S(1)}, s32[32]{0:T(128)}, u32[]{:S(2)}) copy-start(s32[32]{0:T(128)} %get-tuple-element.123) | copy-start | bytes 388
  82.9 3.5 %copy-start.13 = (s32[32]{0:T(128)S(1)}, s32[32]{0:T(128)}, u32[]{:S(2)}) copy-start(s32[32]{0:T(128)} %get-tuple-element.119) | copy-start | bytes 388
  87.9 10.8 %all-to-all-start.1 = ((f32[4,1,512]{2,1,0:T(1,128)}), f32[4,1,512]{2,1,0:T(1,128)S(1)}, u32[]{:S(2)}, u32[]{:S(2)}) async-start(f32[4,1,512]{2,1,0:T(1,128)} %reshape.219), calls=%async_computation.1 | async-start | bytes 16384 | tf_op jit(solution)/shard_map/all_to_all | solution.py:91
  98.7 24.1 %all-to-all-start = ((f32[1,128,2,8,128]{4,3,2,0,1:T(8,128)}), f32[1,128,2,8,128]{4,3,2,0,1:T(8,128)S(1)}, u32[]{:S(2)}, u32[]{:S(2)}) async-start(f32[1,128,2,8,128]{4,3,2,0,1:T(8,128)} %add_bitcast_fusion), calls=%async_computation | async-start | bytes 2097152 | tf_op jit(solution)/shard_map/all_to_all | solution.py:93
where the time goes:
time: 124 us
  local copies, waits for them, and re-layouts  37 us (30%)
  waiting for transfers between devices  22 us (18%)
  other arithmetic  18.4 us (15%)
  blocking collectives  17.7 us (14%)
  starting transfers between devices  14.2 us (11%)
  matrix products  14 us (11%)
    all_to_all x1, waiting for transfers between devices, body(): lax.all_to_all(local_part[2][None], 'seq', split_axis=1, concat_axis=0, t...  18 us
    all_gather x1, blocking collectives, body(): gathered = lax.all_gather(queries, 'seq', axis=0, tiled=True)  17.7 us
    unnamed x42, local copies, waits for them, and re-layouts  9.32 us
    dot_general x4, matrix products, attend(): jnp.einsum('taoz,zah->taoh', softmax_weights.astype(jnp.bfloat16), value_...  9.14 us
    reduce_sum x4, other arithmetic, attend(): row_sum = jnp.sum(softmax_weights, axis=-1)  5.79 us
    all_to_all x1, starting transfers between devices, body(): lax.all_to_all(local_part[1][None], 'seq', split_axis=1, concat_axis=0, t...  5.52 us
    all_to_all x1, starting transfers between devices, body(): lax.all_to_all(local_part[0][None], 'seq', split_axis=1, concat_axis=0, t...  5.17 us
    sort x2, other arithmetic, body(): jnp.argsort((branch_id[:, 0] != branch).astype(jnp.int32), stable=True)  5.07 us
  transfers between devices with their start and end apart: 3, of which 2 were waited for; matrix products, arithmetic and copies ran while one was open for 15% of the time, Pallas kernels for 0%

commit v1 on v0

v1 whole, which is shorter than its diff:
```python
import functools

import jax
import jax.numpy as jnp
from jax import lax
from jax.experimental import pallas as pl
from jax.experimental.pallas import tpu as pltpu
from jax.sharding import PartitionSpec as P

QHEADS = 64
KVHEADS = 8
HEAD_DIM = 128
GROUP = QHEADS // KVHEADS
MESH = pl.DeviceIdType.MESH
LOG2E = 1.4426950408889634
SCALE2 = HEAD_DIM ** (-0.5) * LOG2E
MASKED = -1e30


def attend(q, keys, values, live=None):
    s = lax.dot_general(q, keys, (((1,), (1,)), ((), ())), preferred_element_type=jnp.float32)
    if live is not None:
        s = jnp.where(live, s, MASKED)
    m = jnp.max(s, axis=1, keepdims=True)
    p = jnp.exp2((s - m) * SCALE2).astype(jnp.bfloat16)
    o = jnp.dot(p, values, preferred_element_type=jnp.float32)
    return m, o


def stack_heads(rows):
    return jnp.concatenate(
        [rows[:, h * HEAD_DIM : (h + 1) * HEAD_DIM] for h in range(GROUP)], axis=0
    )


def kernel(
    n,
    kv,
    q_hbm,
    rk_hbm,
    rv_hbm,
    bk_hbm,
    bv_hbm,
    id_ref,
    len_ref,
    out_ref,
    qg,
    rk,
    rv,
    bk,
    bv,
    root_o,
    root_m,
    root_l,
    branch_o,
    part_o,
    part_s,
    recv_o,
    recv_s,
    own_sem,
    load_sem,
    qsend_sem,
    qrecv_sem,
    osend_sem,
    orecv_sem,
    ssend_sem,
    srecv_sem,
):
    me = lax.axis_index("seq")
    rows = q_hbm.shape[0]
    all_rows = n * rows
    width = GROUP * HEAD_DIM
    branches = bk_hbm.shape[0]
    branch_len = bk_hbm.shape[1]
    most = 2 * rows // branches
    slots = branches * most

    barrier = pltpu.get_barrier_semaphore()
    for k in range(1, n):
        pl.semaphore_signal(
            barrier, inc=1, device_id={"seq": lax.rem(me + k, n)}, device_id_type=MESH
        )

    def head_cols(f):
        return pl.ds(f * HEAD_DIM, HEAD_DIM)

    def shard_rows(s):
        return pl.ds(pl.multiple_of(s * rows, rows), rows)

    own, loads_k, loads_v = [], [], []
    for f in range(kv):
        own.append(
            pltpu.make_async_copy(
                q_hbm.at[:, pl.ds(f * width, width)], qg.at[f, shard_rows(me)], own_sem.at[f]
            )
        )
        loads_k.append(pltpu.make_async_copy(rk_hbm.at[:, head_cols(f)], rk.at[f], load_sem.at[0, f, 0]))
        loads_v.append(
            pltpu.make_async_copy(
                rv_hbm.at[:, head_cols(f)], rv.at[f, :, pl.ds(0, HEAD_DIM)], load_sem.at[1, f, 0]
            )
        )
    bloads_k, bloads_v = [], []
    for f in range(kv):
        bloads_k.append(
            [
                pltpu.make_async_copy(
                    bk_hbm.at[b, :, head_cols(f)], bk.at[f, b], load_sem.at[2, f, b]
                )
                for b in range(branches)
            ]
        )
        bloads_v.append(
            [
                pltpu.make_async_copy(
                    bv_hbm.at[b, :, head_cols(f)],
                    bv.at[f, b, :, pl.ds(0, HEAD_DIM)],
                    load_sem.at[3, f, b],
                )
                for b in range(branches)
            ]
        )
    for f in range(kv):
        own[f].start()
    loads_k[0].start()

    pl.semaphore_wait(barrier, n - 1)

    def q_copy(f, s, way, hop, src):
        to = me + 1 if way == 0 else me - 1
        return pltpu.make_async_remote_copy(
            src_ref=src,
            dst_ref=qg.at[f, shard_rows(s)],
            send_sem=qsend_sem.at[f, way, hop],
            recv_sem=qrecv_sem.at[f, s],
            device_id={"seq": to},
            device_id_type=MESH,
        )

    def send_own(f):
        src = q_hbm.at[:, pl.ds(f * width, width)]

        @pl.when(me < n - 1)
        def _():
            q_copy(f, me, 0, 0, src).start()

        @pl.when(me > 0)
        def _():
            q_copy(f, me, 1, 0, src).start()

    def forward(f, hop):
        left, right = me - hop, me + hop

        @pl.when(left >= 0)
        def _():
            block = qg.at[f, shard_rows(left)]
            q_copy(f, left, 0, hop, block).wait_recv()

            @pl.when(me < n - 1)
            def _():
                q_copy(f, left, 0, hop, block).start()

        @pl.when(right < n)
        def _():
            block = qg.at[f, shard_rows(right)]
            q_copy(f, right, 1, hop, block).wait_recv()

            @pl.when(me > 0)
            def _():
                q_copy(f, right, 1, hop, block).start()

    def sent(f, hop):
        left, right = me - hop, me + hop

        @pl.when((left >= 0) & (me < n - 1))
        def _():
            q_copy(f, left, 0, hop, qg.at[f, shard_rows(left)]).wait_send()

        @pl.when((right < n) & (me > 0))
        def _():
            q_copy(f, right, 1, hop, qg.at[f, shard_rows(right)]).wait_send()

    for f in range(kv):
        send_own(f)

    for f in range(kv):
        rv[f, :, HEAD_DIM:] = jnp.ones((rv.shape[1], HEAD_DIM), jnp.bfloat16)
        for b in range(branches):
            bv[f, b, :, HEAD_DIM:] = jnp.ones((branch_len, HEAD_DIM), jnp.bfloat16)
    for f in range(kv):
        if f:
            loads_k[f].start()
        loads_v[f].start()
        for b in range(branches):
            bloads_k[f][b].start()
            bloads_v[f][b].start()

    slot = lax.broadcasted_iota(jnp.int32, (all_rows, slots), 1)
    named = id_ref[...] == me * branches + slot // most
    named_b = jnp.where(named, 1.0, 0.0).astype(jnp.bfloat16)
    tri = jnp.where(
        lax.broadcasted_iota(jnp.int32, (all_rows, all_rows), 0)
        >= lax.broadcasted_iota(jnp.int32, (all_rows, all_rows), 1),
        1.0,
        0.0,
    ).astype(jnp.bfloat16)
    rank = jnp.dot(tri, named_b, preferred_element_type=jnp.float32)
    place = named & (rank == (lax.rem(slot, most) + 1).astype(jnp.float32))
    place_f = jnp.where(place, 1.0, 0.0)
    place_b = place_f.astype(jnp.bfloat16)
    held = jnp.dot(place_b, jnp.ones((slots, HEAD_DIM), jnp.bfloat16), preferred_element_type=jnp.float32)

    lane = lax.broadcasted_iota(jnp.int32, (rows, HEAD_DIM), 1)
    slot_lane = lax.broadcasted_iota(jnp.int32, (most, HEAD_DIM), 1)
    position = lax.broadcasted_iota(jnp.int32, (1, branch_len), 1)

    def o_copy(f, s, src_dev):
        return pltpu.make_async_remote_copy(
            src_ref=part_o.at[f, s],
            dst_ref=recv_o.at[f, src_dev],
            send_sem=osend_sem.at[f, s],
            recv_sem=orecv_sem.at[f, src_dev],
            device_id={"seq": s},
            device_id_type=MESH,
        )

    def s_copy(f, s, src_dev):
        return pltpu.make_async_remote_copy(
            src_ref=part_s.at[f, s],
            dst_ref=recv_s.at[f, src_dev],
            send_sem=ssend_sem.at[f, s],
            recv_sem=srecv_sem.at[f, src_dev],
            device_id={"seq": s},
            device_id_type=MESH,
        )

    own[0].wait()
    for hop in range(1, n):
        forward(0, hop)
    loads_k[0].wait()
    loads_v[0].wait()

    for f in range(kv):
        if f:
            loads_k[f].wait()
            loads_v[f].wait()

        def root_step(s, carry, f=f):
            m, o = attend(stack_heads(qg[f, shard_rows(s)]), rk[f], rv[f])
            ms = jnp.zeros((rows, HEAD_DIM), jnp.float32)
            ls = jnp.ones((rows, HEAD_DIM), jnp.float32)
            for h in range(GROUP):
                part = slice(h * rows, (h + 1) * rows)
                root_o[shard_rows(s), h * HEAD_DIM : (h + 1) * HEAD_DIM] = o[part, :HEAD_DIM]
                ms = jnp.where(lane == h, m[part], ms)
                ls = jnp.where(lane == h, o[part, HEAD_DIM:], ls)
            root_m[shard_rows(s)] = ms
            root_l[shard_rows(s)] = ls
            if f + 1 < kv:

                @pl.when(s > 0)
                def _():
                    forward(f + 1, s)

            return carry

        lax.fori_loop(0, n, root_step, 0)
        if f + 1 < kv:
            own[f + 1].wait()

        picked = lax.dot_general(
            place_b, qg[f], (((0,), (0,)), ((), ())), preferred_element_type=jnp.float32
        ).astype(jnp.bfloat16)
        lses = []
        for b in range(branches):
            bloads_k[f][b].wait()
            bloads_v[f][b].wait()
            live = position < len_ref[me * branches + b]
            m, o = attend(
                stack_heads(picked[b * most : (b + 1) * most]), bk[f, b], bv[f, b], live
            )
            ms = jnp.zeros((most, HEAD_DIM), jnp.float32)
            ls = jnp.ones((most, HEAD_DIM), jnp.float32)
            for h in range(GROUP):
                part = slice(h * most, (h + 1) * most)
                branch_o[b * most : (b + 1) * most, h * HEAD_DIM : (h + 1) * HEAD_DIM] = (
                    o[part, :HEAD_DIM] / o[part, HEAD_DIM:]
                ).astype(jnp.bfloat16)
                ms = jnp.where(slot_lane == h, m[part], ms)
                ls = jnp.where(slot_lane == h, o[part, HEAD_DIM:], ls)
            lses.append(ms * SCALE2 + jnp.log2(ls))
        put_s = jnp.dot(
            place_f,
            jnp.concatenate(lses, axis=0),
            precision=lax.Precision.HIGHEST,
            preferred_element_type=jnp.float32,
        )
        put_s = jnp.where(held > 0.5, put_s, MASKED)
        root_sum = root_l[...]
        root_lse = root_m[...] * SCALE2 + jnp.log2(root_sum)
        top = jnp.maximum(root_lse, put_s)
        root_w = jnp.exp2(root_lse - top)
        branch_w = jnp.exp2(put_s - top)
        total = root_w + branch_w
        joined = top + jnp.log2(total)
        root_m[...] = root_w / (total * root_sum)
        root_l[...] = branch_w / total
        for s in range(n):
            part_s[f, s] = joined[s * rows : (s + 1) * rows]
        put_o = jnp.dot(place_b, branch_o[...], preferred_element_type=jnp.float32)
        for h in range(GROUP):
            cols = slice(h * HEAD_DIM, (h + 1) * HEAD_DIM)
            mixed = (
                root_o[:, cols] * root_m[:, h : h + 1] + put_o[:, cols] * root_l[:, h : h + 1]
            ).astype(jnp.bfloat16)
            for s in range(n):
                part_o[f, s, :, cols] = mixed[s * rows : (s + 1) * rows]
        for k in range(1, n):
            s = lax.rem(me + k, n)
            o_copy(f, s, me).start()
            s_copy(f, s, me).start()
    for f in range(kv):
        for k in range(1, n):
            s = lax.rem(me + k, n)
            o_copy(f, s, s).wait_recv()
            s_copy(f, s, s).wait_recv()
        recv_s[f, me] = part_s[f, me]
        recv_o[f, me] = part_o[f, me]
        lse = [recv_s[f, s] for s in range(n)]
        top = functools.reduce(jnp.maximum, lse)
        weights = [jnp.exp2(x - top) for x in lse]
        total = functools.reduce(jnp.add, weights)
        coefs = [w / total for w in weights]
        for h in range(GROUP):
            cols = slice(h * HEAD_DIM, (h + 1) * HEAD_DIM)
            acc = recv_o[f, 0, :, cols].astype(jnp.float32) * coefs[0][:, h : h + 1]
            for s in range(1, n):
                acc += recv_o[f, s, :, cols].astype(jnp.float32) * coefs[s][:, h : h + 1]
            out_ref[:, f * width + h * HEAD_DIM : f * width + (h + 1) * HEAD_DIM] = acc.astype(
                jnp.bfloat16
            )

    for f in range(kv):
        for hop in range(n - 1):
            sent(f, hop)
        for k in range(1, n):
            s = lax.rem(me + k, n)
            o_copy(f, s, me).wait_send()
            s_copy(f, s, me).wait_send()


def body(n, queries, root_keys, root_values, branch_keys, branch_values, branch_id, doc_len):
    rows = queries.shape[0]
    kv = root_keys.shape[1] // HEAD_DIM
    root_len = root_keys.shape[0]
    branches, branch_len = branch_keys.shape[:2]
    width = GROUP * HEAD_DIM
    all_rows = n * rows
    most = 2 * rows // branches
    slots = branches * most
    any_spec = pl.BlockSpec(memory_space=pl.ANY)
    bf16, f32 = jnp.bfloat16, jnp.float32
    dma = pltpu.SemaphoreType.DMA
    return pl.pallas_call(
        functools.partial(kernel, n, kv),
        out_shape=jax.ShapeDtypeStruct(queries.shape, bf16),
        in_specs=[any_spec] * 5
        + [pl.BlockSpec(memory_space=pltpu.VMEM), pl.BlockSpec(memory_space=pltpu.SMEM)],
        out_specs=pl.BlockSpec(memory_space=pltpu.VMEM),
        scratch_shapes=[
            pltpu.VMEM((kv, all_rows, width), bf16),
            pltpu.VMEM((kv, root_len, HEAD_DIM), bf16),
            pltpu.VMEM((kv, root_len, 2 * HEAD_DIM), bf16),
            pltpu.VMEM((kv, branches, branch_len, HEAD_DIM), bf16),
            pltpu.VMEM((kv, branches, branch_len, 2 * HEAD_DIM), bf16),
            pltpu.VMEM((all_rows, width), f32),
            pltpu.VMEM((all_rows, HEAD_DIM), f32),
            pltpu.VMEM((all_rows, HEAD_DIM), f32),
            pltpu.VMEM((slots, width), bf16),
            pltpu.VMEM((kv, n, rows, width), bf16),
            pltpu.VMEM((kv, n, rows, HEAD_DIM), f32),
            pltpu.VMEM((kv, n, rows, width), bf16),
            pltpu.VMEM((kv, n, rows, HEAD_DIM), f32),
            dma((kv,)),
            dma((4, kv, branches)),
            dma((kv, 2, n)),
            dma((kv, n)),
            dma((kv, n)),
            dma((kv, n)),
            dma((kv, n)),
            dma((kv, n)),
        ],
        compiler_params=pltpu.CompilerParams(
            collective_id=0, has_side_effects=True, vmem_limit_bytes=60 * 1024 * 1024
        ),
    )(queries, root_keys, root_values, branch_keys, branch_values, branch_id, doc_len)


def solution(mesh):
    in_specs = (
        P(("parts", "seq"), "head"),
        P(("parts", "seq"), "head"),
        P(("parts", "seq"), "head"),
        P(("parts", "seq"), None, "head"),
        P(("parts", "seq"), None, "head"),
        P("parts", None),
        P("parts"),
    )
    out_specs = P(("parts", "seq"), "head")
    return jax.shard_map(
        functools.partial(body, mesh.shape["seq"]),
        mesh=mesh,
        in_specs=in_specs,
        out_specs=out_specs,
        check_vma=False,
    )
```

time: 124 us -> 44.3 us (0.36)
  Pallas kernels: 0 us -> 41.1 us
  local copies, waits for them, and re-layouts: 37 us -> 2.96 us
  waiting for transfers between devices: 22 us -> 0 us
  other arithmetic: 18.4 us -> 0 us
  blocking collectives: 17.7 us -> 0 us
  starting transfers between devices: 14.2 us -> 0 us
  matrix products: 14 us -> 0 us
    pallas_call x0 -> x1, Pallas kernels: none -> 41.1 us  [body(): pl.pallas_call(functools.partial(kernel, n, kv), out_shape=jax.ShapeDtype...]
    all_to_all x3 -> x0, waiting for transfers between devices: 22 us -> none  [the longest x1 18 us: body(): lax.all_to_all(local_part[2][None], 'seq', split_axis=1, concat_axis=0, t...]
    all_gather x1 -> x0, blocking collectives: 17.7 us -> none  [body(): gathered = lax.all_gather(queries, 'seq', axis=0, tiled=True)]
    all_to_all x3 -> x0, starting transfers between devices: 14.2 us -> none  [the longest x1 5.52 us: body(): lax.all_to_all(local_part[1][None], 'seq', split_axis=1, concat_axis=0, t...]
    dot_general x8 -> x0, matrix products: 14 us -> none  [the longest x4 9.14 us: attend(): jnp.einsum('taoz,zah->taoh', softmax_weights.astype(jnp.bfloat16), value_...]
    scatter x8 -> x0, local copies, waits for them, and re-layouts: 9.49 us -> none  [the longest x3 3.3 us: body(): branch_part[0].at[target].set(result[0], mode='drop')]
    unnamed x42 -> x2, local copies, waits for them, and re-layouts: 9.32 us -> 2.96 us
    reduce_sum x6 -> x0, other arithmetic: 6.26 us -> none  [the longest x4 5.79 us: attend(): row_sum = jnp.sum(softmax_weights, axis=-1)]
  transfers between devices with their start and end apart: 3 -> 0, of which waited for: 2 -> 0; matrix products, arithmetic and copies ran while one was open for 15% -> 0% of each run, Pallas kernels for 0% -> 0%
where the time goes in v1:
time: 44.3 us; the launch traced here: 44.1 us
  Pallas kernels  41.1 us (93%)
  local copies, waits for them, and re-layouts  2.96 us (7%)
    pallas_call x1, Pallas kernels, body(): pl.pallas_call(functools.partial(kernel, n, kv), out_shape=jax.ShapeDtype...  41.1 us
    unnamed x2, local copies, waits for them, and re-layouts  2.96 us

profile of v1, /device:TPU:0, one launch (start us, length us, event | category | flops | bytes accessed | tf_op | source)
XLA Modules:
  0.0 44.1 jit_solution(17447777353179035473)
XLA Ops:
  0.0 1.4 %copy.8.id_ref = s32[128,1]{1,0:T(8,128)} copy(s32[128,1]{0,1:T(1,128)} %param.12) | data formatting | bytes 1024 | tf_op args[5]
  1.4 41.1 %shard_map.73 = bf16[32,2048]{1,0:T(8,128)(2,1)} custom-call(bf16[32,2048]{1,0:T(8,128)(2,1)} %q_hbm.1, bf16[2048,256]{1,0:T(8,128)(2,1)} %rk_hbm.1, bf16[2048,256]{1,0:T(8,128)(2,1)} %rv_hbm.1, bf16[2,2048,256]{2,1,0:T(8,128)(2,1)} %bk_hbm.1, bf16[2,2048,256]{2,1,0:T(8,128)(2,1)} %bv_hbm.1, s32[128,1]{1,0:T(8,128)} %copy.8.id_ref, s32[8]{0:T(128)} %len_ref.1), custom_call_target="tpu_custom_call" | custom-call | tf_op jit(solution)/shard_map/pallas_call | solution.py:364
  42.5 1.6 %copy.10 = bf16[32,2048]{1,0:T(8,128)(2,1)} copy(bf16[32,2048]{1,0:T(8,128)(2,1)} %shard_map.73) | data formatting | bytes 262144

commit v2 on v1

v2 whole, which is shorter than its diff:
```python
import functools

import jax
import jax.numpy as jnp
from jax import lax
from jax.experimental import pallas as pl
from jax.experimental.pallas import tpu as pltpu
from jax.sharding import PartitionSpec as P

QHEADS = 64
KVHEADS = 8
HEAD_DIM = 128
GROUP = QHEADS // KVHEADS
MESH = pl.DeviceIdType.MESH
LOG2E = 1.4426950408889634
SCALE2 = HEAD_DIM ** (-0.5) * LOG2E
MASKED = -1e30


def attend(q, keys, values, live=None):
    s = lax.dot_general(q, keys, (((1,), (1,)), ((), ())), preferred_element_type=jnp.float32)
    if live is not None:
        s = jnp.where(live, s, MASKED)
    m = jnp.max(s, axis=1, keepdims=True)
    p = jnp.exp2((s - m) * SCALE2).astype(jnp.bfloat16)
    o = jnp.dot(p, values, preferred_element_type=jnp.float32)
    return m, o


def stack_heads(rows):
    return jnp.concatenate(
        [rows[:, h * HEAD_DIM : (h + 1) * HEAD_DIM] for h in range(GROUP)], axis=0
    )


def kernel(
    n,
    kv,
    q_hbm,
    rk_hbm,
    rv_hbm,
    bk_hbm,
    bv_hbm,
    id_ref,
    len_ref,
    out_ref,
    qg,
    rk,
    rv,
    bk,
    bv,
    root_o,
    root_m,
    root_l,
    branch_o,
    part,
    recv,
    own_sem,
    load_sem,
    qsend_sem,
    qrecv_sem,
    psend_sem,
    precv_sem,
):
    me = lax.axis_index("seq")
    rows = q_hbm.shape[0]
    all_rows = n * rows
    width = GROUP * HEAD_DIM
    branches = bk_hbm.shape[0]
    branch_len = bk_hbm.shape[1]
    most = 2 * rows // branches
    slots = branches * most
    has_left, has_right = me > 0, me < n - 1

    barrier = pltpu.get_barrier_semaphore()

    @pl.when(has_left)
    def _():
        pl.semaphore_signal(barrier, inc=1, device_id={"seq": me - 1}, device_id_type=MESH)

    @pl.when(has_right)
    def _():
        pl.semaphore_signal(barrier, inc=1, device_id={"seq": me + 1}, device_id_type=MESH)

    def head_cols(f):
        return pl.ds(f * HEAD_DIM, HEAD_DIM)

    def shard_rows(s):
        return pl.ds(pl.multiple_of(s * rows, rows), rows)

    own, loads_k, loads_v = [], [], []
    for f in range(kv):
        own.append(
            pltpu.make_async_copy(
                q_hbm.at[:, pl.ds(f * width, width)], qg.at[f, shard_rows(me)], own_sem.at[f]
            )
        )
        loads_k.append(
            pltpu.make_async_copy(rk_hbm.at[:, head_cols(f)], rk.at[f], load_sem.at[0, f, 0])
        )
        loads_v.append(
            pltpu.make_async_copy(
                rv_hbm.at[:, head_cols(f)], rv.at[f, :, pl.ds(0, HEAD_DIM)], load_sem.at[1, f, 0]
            )
        )
    bloads_k, bloads_v = [], []
    for f in range(kv):
        bloads_k.append(
            [
                pltpu.make_async_copy(
                    bk_hbm.at[b, :, head_cols(f)], bk.at[f, b], load_sem.at[2, f, b]
                )
                for b in range(branches)
            ]
        )
        bloads_v.append(
            [
                pltpu.make_async_copy(
                    bv_hbm.at[b, :, head_cols(f)],
                    bv.at[f, b, :, pl.ds(0, HEAD_DIM)],
                    load_sem.at[3, f, b],
                )
                for b in range(branches)
            ]
        )
    own[0].start()
    loads_k[0].start()

    for f in range(kv):
        rv[f, :, HEAD_DIM:] = jnp.ones((rv.shape[1], HEAD_DIM), jnp.bfloat16)
        loads_v[f].start()
        if f:
            loads_k[f].start()
            own[f].start()
        for b in range(branches):
            bv[f, b, :, HEAD_DIM:] = jnp.ones((branch_len, HEAD_DIM), jnp.bfloat16)
            bloads_k[f][b].start()
            bloads_v[f][b].start()

    pl.semaphore_wait(barrier, jnp.where(has_left & has_right, 2, 1))

    def q_copy(f, s, way, hop, src):
        return pltpu.make_async_remote_copy(
            src_ref=src,
            dst_ref=qg.at[f, shard_rows(s)],
            send_sem=qsend_sem.at[f, way, hop],
            recv_sem=qrecv_sem.at[f, s],
            device_id={"seq": me + 1 if way == 0 else me - 1},
            device_id_type=MESH,
        )

    def send_own(f):
        src = q_hbm.at[:, pl.ds(f * width, width)]

        @pl.when(has_right)
        def _():
            q_copy(f, me, 0, 0, src).start()

        @pl.when(has_left)
        def _():
            q_copy(f, me, 1, 0, src).start()

    def pass_right(f, hop):
        s = me - hop
        block = qg.at[f, shard_rows(s)]
        q_copy(f, s, 0, hop, block).wait_recv()

        @pl.when(has_right)
        def _():
            q_copy(f, s, 0, hop, block).start()

    def pass_left(f, hop):
        s = me + hop
        block = qg.at[f, shard_rows(s)]
        q_copy(f, s, 1, hop, block).wait_recv()

        @pl.when(has_left)
        def _():
            q_copy(f, s, 1, hop, block).start()

    def forward(f, hop):
        @pl.when(me - hop >= 0)
        def _():
            pass_right(f, hop)

        @pl.when(me + hop < n)
        def _():
            pass_left(f, hop)

    def sent(f, hop):
        left, right = me - hop, me + hop

        @pl.when((left >= 0) & has_right)
        def _():
            q_copy(f, left, 0, hop, qg.at[f, shard_rows(left)]).wait_send()

        @pl.when((right < n) & has_left)
        def _():
            q_copy(f, right, 1, hop, qg.at[f, shard_rows(right)]).wait_send()

    send_own(0)

    slot = lax.broadcasted_iota(jnp.int32, (slots, all_rows), 0)
    named = id_ref[...] == me * branches + slot // most
    named_b = jnp.where(named, 1.0, 0.0).astype(jnp.bfloat16)
    tri = jnp.where(
        lax.broadcasted_iota(jnp.int32, (all_rows, all_rows), 0)
        <= lax.broadcasted_iota(jnp.int32, (all_rows, all_rows), 1),
        1.0,
        0.0,
    ).astype(jnp.bfloat16)
    rank = jnp.dot(named_b, tri, preferred_element_type=jnp.float32)
    pick_f = jnp.where(named & (rank == (lax.rem(slot, most) + 1).astype(jnp.float32)), 1.0, 0.0)
    pick_b = pick_f.astype(jnp.bfloat16)
    place_f = pick_f.T
    place_b = place_f.astype(jnp.bfloat16)
    held = jnp.dot(
        place_b, jnp.ones((slots, HEAD_DIM), jnp.bfloat16), preferred_element_type=jnp.float32
    )

    lane = lax.broadcasted_iota(jnp.int32, (rows, HEAD_DIM), 1)
    all_lane = lax.broadcasted_iota(jnp.int32, (all_rows, HEAD_DIM), 1)
    slot_lane = lax.broadcasted_iota(jnp.int32, (most, HEAD_DIM), 1)
    position = lax.broadcasted_iota(jnp.int32, (1, branch_len), 1)
    side_cols = slice(width, width + HEAD_DIM)

    def split(x, lanes):
        high = x.astype(jnp.bfloat16).astype(jnp.float32)
        rest = x - high
        mid = rest.astype(jnp.bfloat16).astype(jnp.float32)
        low = rest - mid
        return jnp.where(
            lanes < GROUP,
            high,
            jnp.where(
                lanes < 2 * GROUP, pltpu.roll(mid, GROUP, axis=1), pltpu.roll(low, 2 * GROUP, axis=1)
            ),
        ).astype(jnp.bfloat16)

    def whole(x):
        x = x.astype(jnp.float32)
        return (
            x
            + pltpu.roll(x, HEAD_DIM - GROUP, axis=1)
            + pltpu.roll(x, HEAD_DIM - 2 * GROUP, axis=1)
        )

    def merge(f, d, side):
        lse_a = whole(part[f, d, :, side_cols])
        lse_b = whole(recv[f, d, side, :, side_cols])
        top = jnp.maximum(lse_a, lse_b)
        a, b = jnp.exp2(lse_a - top), jnp.exp2(lse_b - top)
        total = a + b
        a, b = a / total, b / total
        for h in range(GROUP):
            cols = slice(h * HEAD_DIM, (h + 1) * HEAD_DIM)
            part[f, d, :, cols] = (
                part[f, d, :, cols].astype(jnp.float32) * a[:, h : h + 1]
                + recv[f, d, side, :, cols].astype(jnp.float32) * b[:, h : h + 1]
            ).astype(jnp.bfloat16)
        part[f, d, :, side_cols] = split(top + jnp.log2(total), lane)

    def p_copy(f, d, side):
        return pltpu.make_async_remote_copy(
            src_ref=part.at[f, d],
            dst_ref=recv.at[f, d, side],
            send_sem=psend_sem.at[f, d],
            recv_sem=precv_sem.at[f, d, side],
            device_id={"seq": me + 1 if side == 0 else me - 1},
            device_id_type=MESH,
        )

    def stage(f, h):
        for side in range(2):

            @pl.when((me if side == 0 else n - 1 - me) == h)
            def _(side=side):
                def one(i, carry):
                    d = n - 1 - i if side == 0 else i

                    @pl.when(h > 0)
                    def _():
                        p_copy(f, d, side).wait_recv()
                        merge(f, d, side)

                    p_copy(f, d, side).start()
                    return carry

                lax.fori_loop(0, n - 1 - h, one, 0)

    def finish(f):
        for side in range(2):

            @pl.when(has_left if side == 0 else has_right)
            def _(side=side):
                p_copy(f, me, side).wait_recv()
                merge(f, me, side)

        out_ref[:, f * width : (f + 1) * width] = part[f, me, :, :width]

    def root(f, s):
        m, o = attend(stack_heads(qg[f, shard_rows(s)]), rk[f], rv[f])
        ms = jnp.zeros((rows, HEAD_DIM), jnp.float32)
        ls = jnp.ones((rows, HEAD_DIM), jnp.float32)
        for h in range(GROUP):
            block = slice(h * rows, (h + 1) * rows)
            root_o[shard_rows(s), h * HEAD_DIM : (h + 1) * HEAD_DIM] = o[block, :HEAD_DIM]
            ms = jnp.where(lane == h, m[block], ms)
            ls = jnp.where(lane == h, o[block, HEAD_DIM:], ls)
        root_m[shard_rows(s)] = ms
        root_l[shard_rows(s)] = ls

    own[0].wait()
    loads_k[0].wait()
    loads_v[0].wait()

    for f in range(kv):
        if f == 0:

            def first_step(j, carry):
                hop, left = (j + 1) // 2, lax.rem(j, 2) == 1
                s = jnp.where(left, me - hop, me + hop)

                @pl.when(left & (s >= 0))
                def _():
                    pass_right(0, hop)

                @pl.when((j > 0) & jnp.logical_not(left) & (s < n))
                def _():
                    pass_left(0, hop)

                if kv > 1:

                    @pl.when(j == 2)
                    def _():
                        send_own(1)

                    @pl.when((j > 2) & jnp.logical_not(left))
                    def _():
                        forward(1, hop - 1)

                @pl.when((s >= 0) & (s < n))
                def _():
                    root(0, s)

                return carry

            lax.fori_loop(0, 2 * n - 1, first_step, 0)
        else:
            own[f].wait()
            loads_k[f].wait()
            loads_v[f].wait()

            def root_step(s, carry, f=f):
                root(f, s)

                @pl.when(s == n - 2)
                def _():
                    stage(f - 1, 1)

                return carry

            lax.fori_loop(0, n, root_step, 0)

        picked = jnp.dot(pick_b, qg[f], preferred_element_type=jnp.float32).astype(jnp.bfloat16)
        lses = []
        for b in range(branches):
            bloads_k[f][b].wait()
            bloads_v[f][b].wait()
            live = position < len_ref[me * branches + b]
            m, o = attend(
                stack_heads(picked[b * most : (b + 1) * most]), bk[f, b], bv[f, b], live
            )
            ms = jnp.zeros((most, HEAD_DIM), jnp.float32)
            ls = jnp.ones((most, HEAD_DIM), jnp.float32)
            for h in range(GROUP):
                block = slice(h * most, (h + 1) * most)
                branch_o[b * most : (b + 1) * most, h * HEAD_DIM : (h + 1) * HEAD_DIM] = (
                    o[block, :HEAD_DIM] / o[block, HEAD_DIM:]
                ).astype(jnp.bfloat16)
                ms = jnp.where(slot_lane == h, m[block], ms)
                ls = jnp.where(slot_lane == h, o[block, HEAD_DIM:], ls)
            lses.append(ms * SCALE2 + jnp.log2(ls))
            if b == 0:
                if f == 0 and kv > 1:
                    forward(1, n - 1)
                elif f > 0:
                    for h in range(2, n - 1):
                        stage(f - 1, h)
        put_s = jnp.dot(
            place_f,
            jnp.concatenate(lses, axis=0),
            precision=lax.Precision.HIGHEST,
            preferred_element_type=jnp.float32,
        )
        put_s = jnp.where(held > 0.5, put_s, MASKED)
        root_sum = root_l[...]
        root_lse = root_m[...] * SCALE2 + jnp.log2(root_sum)
        top = jnp.maximum(root_lse, put_s)
        root_w = jnp.exp2(root_lse - top)
        branch_w = jnp.exp2(put_s - top)
        total = root_w + branch_w
        joined = split(top + jnp.log2(total), all_lane)
        root_m[...] = root_w / (total * root_sum)
        root_l[...] = branch_w / total
        for s in range(n):
            part[f, s, :, side_cols] = joined[s * rows : (s + 1) * rows]
        put_o = jnp.dot(place_b, branch_o[...], preferred_element_type=jnp.float32)
        for h in range(GROUP):
            cols = slice(h * HEAD_DIM, (h + 1) * HEAD_DIM)
            mixed = (
                root_o[:, cols] * root_m[:, h : h + 1] + put_o[:, cols] * root_l[:, h : h + 1]
            ).astype(jnp.bfloat16)
            for s in range(n):
                part[f, s, :, cols] = mixed[s * rows : (s + 1) * rows]
        stage(f, 0)
        if f > 0:
            finish(f - 1)
    for h in range(1, n - 1):
        stage(kv - 1, h)
    finish(kv - 1)

    for f in range(kv):
        for hop in range(n - 1):
            sent(f, hop)
        for k in range(1, n):
            p_copy(f, lax.rem(me + k, n), 0).wait_send()


def body(n, queries, root_keys, root_values, branch_keys, branch_values, branch_id, doc_len):
    rows = queries.shape[0]
    kv = root_keys.shape[1] // HEAD_DIM
    root_len = root_keys.shape[0]
    branches, branch_len = branch_keys.shape[:2]
    width = GROUP * HEAD_DIM
    all_rows = n * rows
    most = 2 * rows // branches
    slots = branches * most
    any_spec = pl.BlockSpec(memory_space=pl.ANY)
    bf16, f32 = jnp.bfloat16, jnp.float32
    dma = pltpu.SemaphoreType.DMA
    return pl.pallas_call(
        functools.partial(kernel, n, kv),
        out_shape=jax.ShapeDtypeStruct(queries.shape, bf16),
        in_specs=[any_spec] * 5
        + [pl.BlockSpec(memory_space=pltpu.VMEM), pl.BlockSpec(memory_space=pltpu.SMEM)],
        out_specs=pl.BlockSpec(memory_space=pltpu.VMEM),
        scratch_shapes=[
            pltpu.VMEM((kv, all_rows, width), bf16),
            pltpu.VMEM((kv, root_len, HEAD_DIM), bf16),
            pltpu.VMEM((kv, root_len, 2 * HEAD_DIM), bf16),
            pltpu.VMEM((kv, branches, branch_len, HEAD_DIM), bf16),
            pltpu.VMEM((kv, branches, branch_len, 2 * HEAD_DIM), bf16),
            pltpu.VMEM((all_rows, width), f32),
            pltpu.VMEM((all_rows, HEAD_DIM), f32),
            pltpu.VMEM((all_rows, HEAD_DIM), f32),
            pltpu.VMEM((slots, width), bf16),
            pltpu.VMEM((kv, n, rows, width + HEAD_DIM), bf16),
            pltpu.VMEM((kv, n, 2, rows, width + HEAD_DIM), bf16),
            dma((kv,)),
            dma((4, kv, branches)),
            dma((kv, 2, n)),
            dma((kv, n)),
            dma((kv, n)),
            dma((kv, n, 2)),
        ],
        compiler_params=pltpu.CompilerParams(
            collective_id=0, has_side_effects=True, vmem_limit_bytes=60 * 1024 * 1024
        ),
    )(queries, root_keys, root_values, branch_keys, branch_values, branch_id.reshape(1, -1), doc_len)


def solution(mesh):
    in_specs = (
        P(("parts", "seq"), "head"),
        P(("parts", "seq"), "head"),
        P(("parts", "seq"), "head"),
        P(("parts", "seq"), None, "head"),
        P(("parts", "seq"), None, "head"),
        P("parts", None),
        P("parts"),
    )
    out_specs = P(("parts", "seq"), "head")
    return jax.shard_map(
        functools.partial(body, mesh.shape["seq"]),
        mesh=mesh,
        in_specs=in_specs,
        out_specs=out_specs,
        check_vma=False,
    )
```

time: 44.3 us -> 44.2 us (level)
  Pallas kernels: 41.1 us -> 42.5 us
  local copies, waits for them, and re-layouts: 2.96 us -> 1.57 us
    unnamed x2 -> x1, local copies, waits for them, and re-layouts: 2.96 us -> 1.57 us
    pallas_call x1, Pallas kernels: 41.1 us -> 42.5 us  [body(): pl.pallas_call(functools.partial(kernel, n, kv), out_shape=jax.ShapeDtype...]
where the time goes in v2:
time: 44.2 us; the launch traced here: 44 us
  Pallas kernels  42.5 us (96%)
  local copies, waits for them, and re-layouts  1.57 us (4%)
    pallas_call x1, Pallas kernels, body(): pl.pallas_call(functools.partial(kernel, n, kv), out_shape=jax.ShapeDtype...  42.5 us
    unnamed x1, local copies, waits for them, and re-layouts  1.57 us

profile of v2, /device:TPU:0, one launch (start us, length us, event | category | flops | bytes accessed | tf_op | source)
XLA Modules:
  0.0 44.0 jit_solution(14346218792877404671)
XLA Ops:
  0.0 42.5 %shard_map.73 = bf16[32,2048]{1,0:T(8,128)(2,1)} custom-call(bf16[32,2048]{1,0:T(8,128)(2,1)} %q_hbm.1, bf16[2048,256]{1,0:T(8,128)(2,1)} %rk_hbm.1, bf16[2048,256]{1,0:T(8,128)(2,1)} %rv_hbm.1, bf16[2,2048,256]{2,1,0:T(8,128)(2,1)} %bk_hbm.1, bf16[2,2048,256]{2,1,0:T(8,128)(2,1)} %bv_hbm.1, s32[1,128]{1,0:T(1,128)} %bitcast.1, s32[8]{0:T(128)} %len_ref.1), custom_call_target="tpu_custom_call" | custom-call | tf_op jit(solution)/shard_map/pallas_call | solution.py:442
  42.5 1.6 %copy.9 = bf16[32,2048]{1,0:T(8,128)(2,1)} copy(bf16[32,2048]{1,0:T(8,128)(2,1)} %shard_map.73) | data formatting | bytes 262144

commit v3 on v2

--- a/solution.py
+++ b/solution.py
@@ -15,15 +15,30 @@
 LOG2E = 1.4426950408889634
 SCALE2 = HEAD_DIM ** (-0.5) * LOG2E
 MASKED = -1e30
+KEY_BLOCK = 512
 
 
 def attend(q, keys, values, live=None):
-    s = lax.dot_general(q, keys, (((1,), (1,)), ((), ())), preferred_element_type=jnp.float32)
-    if live is not None:
-        s = jnp.where(live, s, MASKED)
-    m = jnp.max(s, axis=1, keepdims=True)
-    p = jnp.exp2((s - m) * SCALE2).astype(jnp.bfloat16)
-    o = jnp.dot(p, values, preferred_element_type=jnp.float32)
+    size = min(KEY_BLOCK, keys.shape[0])
+    blocks = [slice(i, i + size) for i in range(0, keys.shape[0], size)]
+    scores = []
+    for block in blocks:
+        s = lax.dot_general(
+            q, keys[block], (((1,), (1,)), ((), ())), preferred_element_type=jnp.float32
+        )
+        if live is not None:
+            s = jnp.where(live[:, block], s, MASKED)
+        scores.append(s)
+    tops, sums = [], []
+    for block, s in zip(blocks, scores):
+        t = jnp.max(s, axis=1, keepdims=True)
+        p = jnp.exp2((s - t) * SCALE2).astype(jnp.bfloat16)
+        tops.append(t)
+        sums.append(jnp.dot(p, values[block], preferred_element_type=jnp.float32))
+    m = functools.reduce(jnp.maximum, tops)
+    o = functools.reduce(
+        jnp.add, [x * jnp.exp2((t - m) * SCALE2) for x, t in zip(sums, tops)]
+    )
     return m, o
 
 
@@ -245,58 +260,35 @@
             + pltpu.roll(x, HEAD_DIM - 2 * GROUP, axis=1)
         )
 
-    def merge(f, d, side):
-        lse_a = whole(part[f, d, :, side_cols])
-        lse_b = whole(recv[f, d, side, :, side_cols])
-        top = jnp.maximum(lse_a, lse_b)
-        a, b = jnp.exp2(lse_a - top), jnp.exp2(lse_b - top)
-        total = a + b
-        a, b = a / total, b / total
+    def a_copy(f, d, src):
+        return pltpu.make_async_remote_copy(
+            src_ref=part.at[f, d],
+            dst_ref=recv.at[f, src],
+            send_sem=psend_sem.at[f, d],
+            recv_sem=precv_sem.at[f, src],
+            device_id={"seq": d},
+            device_id_type=MESH,
+        )
+
+    def send(f):
+        for k in range(1, n):
+            a_copy(f, lax.rem(me + k, n), me).start()
+
+    def finish(f):
+        for k in range(1, n):
+            a_copy(f, me, lax.rem(me + k, n)).wait_recv()
+        recv[f, me] = part[f, me]
+        lse = [whole(recv[f, s, :, side_cols]) for s in range(n)]
+        top = functools.reduce(jnp.maximum, lse)
+        weights = [jnp.exp2(x - top) for x in lse]
+        total = functools.reduce(jnp.add, weights)
+        coefs = [w / total for w in weights]
         for h in range(GROUP):
             cols = slice(h * HEAD_DIM, (h + 1) * HEAD_DIM)
-            part[f, d, :, cols] = (
-                part[f, d, :, cols].astype(jnp.float32) * a[:, h : h + 1]
-                + recv[f, d, side, :, cols].astype(jnp.float32) * b[:, h : h + 1]
-            ).astype(jnp.bfloat16)
-        part[f, d, :, side_cols] = split(top + jnp.log2(total), lane)
-
-    def p_copy(f, d, side):
-        return pltpu.make_async_remote_copy(
-            src_ref=part.at[f, d],
-            dst_ref=recv.at[f, d, side],
-            send_sem=psend_sem.at[f, d],
-            recv_sem=precv_sem.at[f, d, side],
-            device_id={"seq": me + 1 if side == 0 else me - 1},
-            device_id_type=MESH,
-        )
-
-    def stage(f, h):
-        for side in range(2):
-
-            @pl.when((me if side == 0 else n - 1 - me) == h)
-            def _(side=side):
-                def one(i, carry):
-                    d = n - 1 - i if side == 0 else i
-
-                    @pl.when(h > 0)
-                    def _():
-                        p_copy(f, d, side).wait_recv()
-                        merge(f, d, side)
-
-                    p_copy(f, d, side).start()
-                    return carry
-
-                lax.fori_loop(0, n - 1 - h, one, 0)
-
-    def finish(f):
-        for side in range(2):
-
-            @pl.when(has_left if side == 0 else has_right)
-            def _(side=side):
-                p_copy(f, me, side).wait_recv()
-                merge(f, me, side)
-
-        out_ref[:, f * width : (f + 1) * width] = part[f, me, :, :width]
+            acc = recv[f, 0, :, cols].astype(jnp.float32) * coefs[0][:, h : h + 1]
+            for s in range(1, n):
+                acc += recv[f, s, :, cols].astype(jnp.float32) * coefs[s][:, h : h + 1]
+            out_ref[:, f * width + h * HEAD_DIM : f * width + (h + 1) * HEAD_DIM] = acc.astype(jnp.bfloat16)
 
     def root(f, s):
         m, o = attend(stack_heads(qg[f, shard_rows(s)]), rk[f], rv[f])
@@ -353,11 +345,6 @@
 
             def root_step(s, carry, f=f):
                 root(f, s)
-
-                @pl.when(s == n - 2)
-                def _():
-                    stage(f - 1, 1)
-
                 return carry
 
             lax.fori_loop(0, n, root_step, 0)
@@ -384,9 +371,6 @@
             if b == 0:
                 if f == 0 and kv > 1:
                     forward(1, n - 1)
-                elif f > 0:
-                    for h in range(2, n - 1):
-                        stage(f - 1, h)
         put_s = jnp.dot(
             place_f,
             jnp.concatenate(lses, axis=0),
@@ -413,18 +397,16 @@
             ).astype(jnp.bfloat16)
             for s in range(n):
                 part[f, s, :, cols] = mixed[s * rows : (s + 1) * rows]
-        stage(f, 0)
+        send(f)
         if f > 0:
             finish(f - 1)
-    for h in range(1, n - 1):
-        stage(kv - 1, h)
     finish(kv - 1)
 
     for f in range(kv):
         for hop in range(n - 1):
             sent(f, hop)
         for k in range(1, n):
-            p_copy(f, lax.rem(me + k, n), 0).wait_send()
+            a_copy(f, lax.rem(me + k, n), me).wait_send()
 
 
 def body(n, queries, root_keys, root_values, branch_keys, branch_values, branch_id, doc_len):
@@ -456,13 +438,13 @@
             pltpu.VMEM((all_rows, HEAD_DIM), f32),
             pltpu.VMEM((slots, width), bf16),
             pltpu.VMEM((kv, n, rows, width + HEAD_DIM), bf16),
-            pltpu.VMEM((kv, n, 2, rows, width + HEAD_DIM), bf16),
+            pltpu.VMEM((kv, n, rows, width + HEAD_DIM), bf16),
             dma((kv,)),
             dma((4, kv, branches)),
             dma((kv, 2, n)),
             dma((kv, n)),
             dma((kv, n)),
-            dma((kv, n, 2)),
+            dma((kv, n)),
         ],
         compiler_params=pltpu.CompilerParams(
             collective_id=0, has_side_effects=True, vmem_limit_bytes=60 * 1024 * 1024

time: 44.2 us -> 34.3 us (0.78)
  Pallas kernels: 42.5 us -> 32.6 us
    pallas_call x1, Pallas kernels: 42.5 us -> 32.6 us  [body(): pl.pallas_call(functools.partial(kernel, n, kv), out_shape=jax.ShapeDtype...]
where the time goes in v3:
time: 34.3 us; the launch traced here: 34.2 us
  Pallas kernels  32.6 us (95%)
  local copies, waits for them, and re-layouts  1.57 us (5%)
    pallas_call x1, Pallas kernels, body(): pl.pallas_call(functools.partial(kernel, n, kv), out_shape=jax.ShapeDtype...  32.6 us
    unnamed x1, local copies, waits for them, and re-layouts  1.57 us

profile of v3, /device:TPU:0, one launch (start us, length us, event | category | flops | bytes accessed | tf_op | source)
XLA Modules:
  0.0 34.2 jit_solution(1441965705342554849)
XLA Ops:
  0.0 32.6 %shard_map.73 = bf16[32,2048]{1,0:T(8,128)(2,1)} custom-call(bf16[32,2048]{1,0:T(8,128)(2,1)} %q_hbm.1, bf16[2048,256]{1,0:T(8,128)(2,1)} %rk_hbm.1, bf16[2048,256]{1,0:T(8,128)(2,1)} %rv_hbm.1, bf16[2,2048,256]{2,1,0:T(8,128)(2,1)} %bk_hbm.1, bf16[2,2048,256]{2,1,0:T(8,128)(2,1)} %bv_hbm.1, s32[1,128]{1,0:T(1,128)} %bitcast.1, s32[8]{0:T(128)} %len_ref.1), custom_call_target="tpu_custom_call" | custom-call | tf_op jit(solution)/shard_map/pallas_call | solution.py:424
  32.6 1.6 %copy.9 = bf16[32,2048]{1,0:T(8,128)(2,1)} copy(bf16[32,2048]{1,0:T(8,128)(2,1)} %shard_map.73) | data formatting | bytes 262144
